TPU v7x, 32 devices: a whole 2x2x4 slice. The times are simulated.
32 devices in a mesh: row: 4 (over y, core), col: 8 (over z, x).
Axes of the slice: x: 2, y: 2, z: 4, core: 2. Of those that a mesh axis runs over, the one named last changes fastest.
Arguments:
- quant_acts: bfloat16 [1024, 8192], P('col', 'row'), may hold values from -6 to 6
- full_acts: bfloat16 [1024, 8192], P('col', 'row'), may hold values from -6 to 6
Outputs:
- hessian: float32 [8192, 8192], P('row', 'col')
- cross_term: float32 [8192, 8192], P('row', 'col')
All inputs are finite; a program needn't handle non-finite values.
Results may differ from a plain program's by a relative error of at most 0.0028.
Values may be sent and summed in bfloat16 or wider, within the bound.
No kernel may reach another device: no remote copies, remote signals or barrier semaphores. Data moves between devices by JAX's collectives and lax.ppermute only.
A program may use at most 64 MiB of HBM per device.

v0:
```python
import jax
import jax.numpy as jnp
from jax import lax
from jax.sharding import PartitionSpec as P


def transposed(left_side, right_side):
    return lax.dot_general(
        left_side, right_side, (((0,), (0,)), ((), ())), preferred_element_type=jnp.float32
    )


def local(quant_acts, full_acts):
    deltas = (full_acts.astype(jnp.float32) - quant_acts.astype(jnp.float32)).astype(jnp.bfloat16)
    slab_wide = lax.all_gather(quant_acts, "row", axis=1, tiled=True)
    column_ops = lax.all_to_all(slab_wide, "col", split_axis=1, concat_axis=0, tiled=True)
    total_tokens = column_ops.shape[0]
    hessian = transposed(lax.all_gather(quant_acts, "col", axis=0, tiled=True), column_ops)
    cross_term = transposed(lax.all_gather(deltas, "col", axis=0, tiled=True), column_ops)
    scale = 1.0 / total_tokens
    return (hessian * scale, cross_term * scale)


def solution(mesh):
    return jax.shard_map(
        local,
        mesh=mesh,
        in_specs=(P("col", "row"), P("col", "row")),
        out_specs=(P("row", "col"), P("row", "col")),
        check_vma=False,
    )
```

profile of v0, /device:TPU:0, one launch (start us, length us, event | category | flops | bytes accessed | tf_op | source)
XLA Modules:
  0.0 229.3 jit_solution(12659035021333383874)
XLA Ops:
  7.2 0.0 all-gather.6.cloned.1.call-start
  7.2 2.0 copy.4
  9.3 0.0 all-gather.6.cloned.1.call-update
  9.3 0.0 all-gather.8.cloned.1.call-start
  9.3 2.1 subtract_convert_fusion
  11.5 0.0 all-gather.8.cloned.1.call-update
  11.5 0.0 all-gather.4.cloned.1.call-start
  11.5 0.7 all-gather.4.cloned.1.call-update
  12.2 23.2 %all-gather.6.cloned.1.call-done = bf16[128,8192]{0,1:T(8,128)(2,1)} async-done(((bf16[128,2048]{0,1:T(8,128)(2,1)}), bf16[128,8192]{0,1:T(8,128)(2,1)}) %all-gather.6.cloned.1.call-update) | async-done | bytes 2097168 | tf_op jit(solution)/shard_map/all_gather | solution.py:15
  35.4 90.8 %all_to_all.19 = bf16[128,8,1024]{0,2,1:T(8,128)(2,1)S(1)} all-to-all(bf16[128,8,1024]{0,2,1:T(8,128)(2,1)} %bitcast.8), channel_id=1, replica_groups=mesh['row'=4,'col'=8] {'col'}, dimensions={1} | all-to-all | bytes 4194304 | tf_op jit(solution)/shard_map/all_to_all | solution.py:16
  126.3 2.6 %copy.5 = bf16[8,128,1024]{2,1,0:T(8,128)(2,1)} copy(bf16[8,128,1024]{1,2,0:T(8,128)(2,1)S(1)} %bitcast.7) | data formatting | bytes 4194304 | tf_op jit(solution)/shard_map/all_to_all | solution.py:16
  128.8 11.7 %all-gather.8.cloned.1.call-done = bf16[1024,2048]{1,0:T(8,128)(2,1)} async-done(((bf16[128,2048]{1,0:T(8,128)(2,1)}), bf16[1024,2048]{1,0:T(8,128)(2,1)}) %all-gather.8.cloned.1.call-update) | async-done | bytes 4194320 | tf_op jit(solution)/shard_map/all_gather | solution.py:19
  140.6 0.0 copy-start
  140.6 11.0 %convolution_multiply_fusion = f32[2048,1024]{1,0:T(8,128)} fusion(bf16[1024,2048]{1,0:T(8,128)(2,1)} %all-gather.8.cloned.1.call-done, bf16[1024,1024]{1,0:T(8,128)(2,1)} %bitcast.9), kind=kOutput, calls=%fused_computation | convolution fusion | flops 4297064448 | bytes 14680064 | tf_op jit(solution)/shard_map/dot_general | solution.py:8
  151.5 62.2 %all-gather.4.cloned.1.call-done = bf16[1024,2048]{1,0:T(8,128)(2,1)} async-done(((bf16[128,2048]{1,0:T(8,128)(2,1)}), bf16[1024,2048]{1,0:T(8,128)(2,1)}) %all-gather.4.cloned.1.call-update) | async-done | bytes 4194320 | tf_op jit(solution)/shard_map/all_gather | solution.py:18
  213.8 0.0 copy-done
  213.8 9.0 %convolution_multiply_fusion.1 = f32[2048,1024]{1,0:T(8,128)} fusion(bf16[1024,2048]{1,0:T(8,128)(2,1)} %all-gather.4.cloned.1.call-done, bf16[1024,1024]{1,0:T(8,128)(2,1)S(1)} %bitcast.10), kind=kOutput, calls=%fused_computation.1 | convolution fusion | flops 4297064448 | bytes 14680064 | tf_op jit(solution)/shard_map/dot_general | solution.py:8
Async XLA Ops:
  7.2 28.3 %all-gather.6.cloned.1.call-start = ((), (), s32[]{:S(2)}) async-start(), calls=%async_computation.2 | async-start | bytes 2621440 | tf_op jit(solution)/shard_map/all_gather | solution.py:15
  9.3 131.3 %all-gather.8.cloned.1.call-start = ((), (), s32[]{:S(2)}) async-start(), calls=%async_computation.3 | async-start | bytes 4718592 | tf_op jit(solution)/shard_map/all_gather | solution.py:19
  11.5 202.3 %all-gather.4.cloned.1.call-start = ((), (), s32[]{:S(2)}) async-start(), calls=%async_computation.1 | async-start | bytes 4718592 | tf_op jit(solution)/shard_map/all_gather | solution.py:18
  140.6 73.2 %copy-start = (bf16[8,128,1024]{2,1,0:T(8,128)(2,1)S(1)}, bf16[8,128,1024]{2,1,0:T(8,128)(2,1)}, u32[]{:S(2)}) copy-start(bf16[8,128,1024]{2,1,0:T(8,128)(2,1)} %copy.5) | copy-start | bytes 6291460
Sparse Core Ops, SparseCore 0:
  10.1 25.2 all-gather.5
  37.6 102.9 all-gather.7
  142.7 71.0 all-gather.3
where the time goes:
time: 230 us; the launch traced here: 229 us
  waiting for transfers between devices  97.9 us (43%)
  blocking collectives  90.8 us (39%)
  matrix products  20 us (9%)
  between operations  13.7 us (6%)
  local copies, waits for them, and re-layouts  4.63 us (2%)
    all_to_all x1, blocking collectives, local(): lax.all_to_all(slab_wide, 'col', split_axis=1, concat_axis=0, tiled=True)  90.8 us
    all_gather x1, waiting for transfers between devices, local(): lax.all_gather(quant_acts, 'col', axis=0, tiled=True)  62.2 us
    all_gather x1, waiting for transfers between devices, local(): slab_wide = lax.all_gather(quant_acts, 'row', axis=1, tiled=True)  23.2 us
    dot_general x2, matrix products, transposed(): lax.dot_general(left_side, right_side, (((0,), (0,)), ((), ())), preferre...  20 us
    all_gather x1, waiting for transfers between devices, local(): lax.all_gather(deltas, 'col', axis=0, tiled=True)  11.7 us
  transfers between devices with their start and end apart: 3, of which 3 were waited for; matrix products, arithmetic and copies ran while one was open for 7% of the time, Pallas kernels for 0%

commit v1 on v0

--- a/solution.py
+++ b/solution.py
@@ -13,7 +13,10 @@
 def local(quant_acts, full_acts):
     deltas = (full_acts.astype(jnp.float32) - quant_acts.astype(jnp.float32)).astype(jnp.bfloat16)
     slab_wide = lax.all_gather(quant_acts, "row", axis=1, tiled=True)
-    column_ops = lax.all_to_all(slab_wide, "col", split_axis=1, concat_axis=0, tiled=True)
+    column_ops = jnp.concatenate(
+        lax.all_to_all(jnp.stack(jnp.split(slab_wide, lax.axis_size("col"), axis=1)), "col", 0, 0),
+        axis=0,
+    )
     total_tokens = column_ops.shape[0]
     hessian = transposed(lax.all_gather(quant_acts, "col", axis=0, tiled=True), column_ops)
     cross_term = transposed(lax.all_gather(deltas, "col", axis=0, tiled=True), column_ops)

time: 230 us -> 235 us (1.022)
  local copies, waits for them, and re-layouts: 4.63 us -> 17.1 us
  waiting for transfers between devices: 97.9 us -> 86.7 us
  blocking collectives: 90.8 us -> 96.7 us
    all_gather x1, waiting for transfers between devices: 62.2 us -> 5.82 us  [local(): lax.all_gather(quant_acts, 'col', axis=0, tiled=True)]
    all_gather x1, waiting for transfers between devices: 11.7 us -> 55.5 us  [local(): lax.all_gather(deltas, 'col', axis=0, tiled=True)]
    unnamed x3 -> x8, local copies, waits for them, and re-layouts: 2.05 us -> 16.1 us
    all_to_all x1, blocking collectives: 90.8 us -> 96.7 us  [local(): lax.all_to_all(jnp.stack(jnp.split(slab_wide, lax.axis_size('col'), axis=...]
    all_to_all x1 -> x0, local copies, waits for them, and re-layouts: 2.58 us -> none  [local(): lax.all_to_all(slab_wide, 'col', split_axis=1, concat_axis=0, tiled=True)]
  transfers between devices with their start and end apart: 3 -> 3, of which waited for: 3 -> 3; matrix products, arithmetic and copies ran while one was open for 7% -> 12% of each run, Pallas kernels for 0% -> 0%
where the time goes in v1:
time: 235 us
  blocking collectives  96.7 us (41%)
  waiting for transfers between devices  86.7 us (37%)
  matrix products  18 us (8%)
  local copies, waits for them, and re-layouts  17.1 us (7%)
  between operations  13.8 us (6%)
    all_to_all x1, blocking collectives, local(): lax.all_to_all(jnp.stack(jnp.split(slab_wide, lax.axis_size('col'), axis=...  96.7 us
    all_gather x1, waiting for transfers between devices, local(): lax.all_gather(deltas, 'col', axis=0, tiled=True)  55.5 us
    all_gather x1, waiting for transfers between devices, local(): slab_wide = lax.all_gather(quant_acts, 'row', axis=1, tiled=True)  24 us
    dot_general x2, matrix products, transposed(): lax.dot_general(left_side, right_side, (((0,), (0,)), ((), ())), preferre...  18 us
    unnamed x8, local copies, waits for them, and re-layouts  16.1 us
    all_gather x1, waiting for transfers between devices, local(): lax.all_gather(quant_acts, 'col', axis=0, tiled=True)  5.82 us
  transfers between devices with their start and end apart: 3, of which 3 were waited for; matrix products, arithmetic and copies ran while one was open for 12% of the time, Pallas kernels for 0%

profile of v1, /device:TPU:0, one launch (start us, length us, event | category | flops | bytes accessed | tf_op | source)
XLA Modules:
  0.0 234.5 jit_solution(18279411959545005860)
XLA Ops:
  7.2 0.0 all-gather.4.cloned.1.call-start
  7.2 0.7 all-gather.4.cloned.1.call-update
  7.9 0.0 all-gather.6.cloned.1.call-start
  7.9 0.7 all-gather.6.cloned.1.call-update
  8.6 0.0 all-gather.8.cloned.1.call-start
  8.7 2.1 subtract_convert_fusion
  10.8 0.0 all-gather.8.cloned.1.call-update
  10.9 24.0 %all-gather.4.cloned.1.call-done = bf16[128,8192]{1,0:T(8,128)(2,1)} async-done(((bf16[128,2048]{1,0:T(8,128)(2,1)}), bf16[128,8192]{1,0:T(8,128)(2,1)}) %all-gather.4.cloned.1.call-update) | async-done | bytes 2097168 | tf_op jit(solution)/shard_map/all_gather | solution.py:15
  34.9 1.0 fusion.7
  35.8 1.0 fusion.6
  36.8 1.0 fusion.5
  37.8 1.0 fusion.4
  38.7 1.0 fusion.3
  39.7 1.0 fusion.2
  40.7 1.0 fusion.1
  41.7 1.0 fusion
  42.6 96.7 %all_to_all.5 = bf16[8,128,1024]{2,1,0:T(8,128)(2,1)S(1)} all-to-all(bf16[8,128,1024]{2,1,0:T(8,128)(2,1)S(1)} %fusion), channel_id=1, replica_groups=mesh['row'=4,'col'=8] {'col'}, dimensions={0} | all-to-all | bytes 4194304 | tf_op jit(solution)/shard_map/all_to_all | solution.py:17
  139.3 5.8 %all-gather.6.cloned.1.call-done = bf16[1024,2048]{1,0:T(8,128)(2,1)} async-done(((bf16[128,2048]{1,0:T(8,128)(2,1)}), bf16[1024,2048]{1,0:T(8,128)(2,1)}) %all-gather.6.cloned.1.call-update) | async-done | bytes 4194320 | tf_op jit(solution)/shard_map/all_gather | solution.py:21
  145.2 9.0 %multiply_bitcast_fusion = f32[2048,1024]{0,1:T(8,128)} fusion(bf16[1024,1024]{1,0:T(8,128)(2,1)S(1)} %bitcast.39, bf16[1024,2048]{1,0:T(8,128)(2,1)} %all-gather.6.cloned.1.call-done), kind=kOutput, calls=%fused_computation | convolution fusion | flops 4297064448 | bytes 14680064 | tf_op jit(solution)/shard_map/dot_general | solution.py:8
  154.2 9.3 %copy.4 = f32[2048,1024]{1,0:T(8,128)} copy(f32[2048,1024]{0,1:T(8,128)} %multiply_bitcast_fusion) | data formatting | bytes 16777216
  163.5 55.5 %all-gather.8.cloned.1.call-done = bf16[1024,2048]{1,0:T(8,128)(2,1)} async-done(((bf16[128,2048]{1,0:T(8,128)(2,1)}), bf16[1024,2048]{1,0:T(8,128)(2,1)}) %all-gather.8.cloned.1.call-update) | async-done | bytes 4194320 | tf_op jit(solution)/shard_map/all_gather | solution.py:22
  219.0 9.0 %convolution_multiply_fusion = f32[2048,1024]{1,0:T(8,128)} fusion(bf16[1024,2048]{1,0:T(8,128)(2,1)} %all-gather.8.cloned.1.call-done, bf16[1024,1024]{1,0:T(8,128)(2,1)S(1)} %bitcast.40), kind=kOutput, calls=%fused_computation.1 | convolution fusion | flops 4297064448 | bytes 14680064 | tf_op jit(solution)/shard_map/dot_general | solution.py:8
Async XLA Ops:
  7.2 27.7 %all-gather.4.cloned.1.call-start = ((), (), s32[]{:S(2)}) async-start(), calls=%async_computation.1 | async-start | bytes 2621440 | tf_op jit(solution)/shard_map/all_gather | solution.py:15
  7.9 137.3 %all-gather.6.cloned.1.call-start = ((), (), s32[]{:S(2)}) async-start(), calls=%async_computation.2 | async-start | bytes 4718592 | tf_op jit(solution)/shard_map/all_gather | solution.py:21
  8.6 210.4 %all-gather.8.cloned.1.call-start = ((), (), s32[]{:S(2)}) async-start(), calls=%async_computation.3 | async-start | bytes 4718592 | tf_op jit(solution)/shard_map/all_gather | solution.py:22
Sparse Core Ops, SparseCore 0:
  9.5 25.2 all-gather.3
  37.0 108.1 all-gather.5
  147.3 71.6 all-gather.7
